TPU v7x, 32 devices: a whole 2x2x4 slice. The times are simulated.
32 devices in a mesh: basin: 4 (over x, core), tile: 8 (over z, y).
Axes of the slice: x: 2, y: 2, z: 4, core: 2. Of those that a mesh axis runs over, the one named last changes fastest.
Arguments:
- ocean_fields: bfloat16 [128, 24, 24, 256], P(('basin', 'tile')), may hold values from -6 to 6
- slot_tiles: int32 [128], P(('basin', 'tile')), may hold values from -1 to 31, as said below
- side_sources: int32 [128, 4], P(('basin', 'tile')), may hold values from -1 to 31, as said below
- corner_sources: int32 [128, 4], P(('basin', 'tile')), may hold values from -1 to 31, as said below
- side_sends: int32 [32, 8, 2], P(('basin', 'tile')), may hold values from -1 to 15, as said below
- corner_sends: int32 [32, 8, 2], P(('basin', 'tile')), may hold values from -1 to 15, as said below
- depth_kernel: bfloat16 [49, 256], replicated, may hold values from -0.875 to 0.875
- expand_weight: bfloat16 [256, 1024], replicated, may hold values from -0.375 to 0.375
- reduce_weight: bfloat16 [1024, 256], replicated, may hold values from -0.1875 to 0.1875
- field_cotangent: bfloat16 [128, 24, 24, 256], P(('basin', 'tile')), may hold values from -6 to 6
Outputs:
- next_fields: bfloat16 [128, 24, 24, 256], P(('basin', 'tile'))
- field_grad: bfloat16 [128, 24, 24, 256], P(('basin', 'tile'))
- kernel_grad: float32 [49, 256], replicated
- expand_grad: float32 [256, 1024], replicated
- reduce_grad: float32 [1024, 256], replicated
Inputs may be any that keep to these rules, and one draw needn't show every extreme that they name: `slot_tiles`: each ocean position of a basin is named by exactly one slot of that basin's devices and land positions by none; -1 marks an empty slot. In every basin some device has all 4 slots filled. `side_sources`: an entry is -1 where the neighbouring position is land or beyond the band's first or last tile row; otherwise it names the neighbour's edge record that faces the slot, the band closing in longitude. Slots that are empty have -1 everywhere. `corner_sources`: as side_sources, for the diagonal neighbours and the corner that faces the slot. `side_sends`: [device, peer, k] is the own edge record that is the k-th record for that peer of the same basin, or -1; each record sent is read by exactly one entry of the peer's side_sources, and every such entry is sent. No device sends to itself. In every basin some pair of devices uses all 2 positions. `corner_sends`: as side_sends, for the corner records and corner_sources.
All inputs are finite; a program needn't handle non-finite values.
Results may differ from a plain program's by a relative error of at most 0.006.
Values may be sent and summed in bfloat16 or wider, within the bound.
No kernel may reach another device: no remote copies, remote signals or barrier semaphores. Data moves between devices by JAX's collectives and lax.ppermute only.
A program may use at most 128 MiB of HBM per device.

v0:
```python
import functools
import math

import jax
import jax.numpy as jnp
from jax import lax
from jax.experimental import pallas as pl
from jax.experimental.pallas import tpu as pltpu
from jax.sharding import PartitionSpec as P


KERNEL = 7
TAPS = KERNEL * KERNEL
RIM = 3
LANES = 128
COL0 = 8
LN_EPS = 1e-06
F32 = jnp.float32
BF16 = jnp.bfloat16
VMEM_LIMIT = 60 * 1024 * 1024


def mxu(lhs, rhs, lhs_dim, rhs_dim):
    return lax.dot_general(
        lhs, rhs, (((lhs_dim,), (rhs_dim,)), ((), ())), preferred_element_type=F32
    )


def gelu_parts(pre):
    cdf = 0.5 * (1.0 + lax.erf(pre * (1.0 / math.sqrt(2.0))))
    density = jnp.exp(-0.5 * pre * pre) * (1.0 / math.sqrt(2.0 * math.pi))
    return pre * cdf, cdf + pre * density


def live_factor(slot_ref, slot):
    return jnp.where(slot_ref[slot] >= 0, 1.0, 0.0).astype(F32)


def own_records(cells, side, corner, base, edge, slots):
    area = edge * edge
    rim_rows = RIM * edge
    far = edge - RIM
    for grp in range(cells.shape[0]):
        for s in range(slots):
            at = base + 4 * s
            start = s * area
            side[at, grp] = cells[grp, start : start + rim_rows]
            side[at + 1, grp] = cells[grp, start + area - rim_rows : start + area]
            for c in range(RIM):
                rows = slice(c * edge, (c + 1) * edge)
                side[at + 2, grp, rows] = cells[grp, pl.ds(start + c, edge, stride=edge)]
                side[at + 3, grp, rows] = cells[grp, pl.ds(start + far + c, edge, stride=edge)]
            for e in range(4):
                row0 = far if e // 2 else 0
                col0 = far if e % 2 else 0
                for r in range(RIM):
                    first = start + (row0 + r) * edge + col0
                    corner[at + e, grp, RIM * r : RIM * r + RIM] = cells[grp, first : first + RIM]


def send_records(send, side, corner, side_sends, corner_sends, zero_at, base=0):
    peers = send.shape[0]
    groups = side.shape[1]
    cap = side_sends.shape[2]

    def one_peer(p, carry):
        for grp in range(groups):
            pieces = []
            for table, sends in ((side, side_sends), (corner, corner_sends)):
                for k in range(cap):
                    code = sends[0, p, k]
                    pieces.append(table[jnp.where(code < 0, zero_at, code + base), grp])
            block = jnp.concatenate(pieces, axis=0)
            send[p, :, grp * LANES : (grp + 1) * LANES] = block.astype(BF16)
        return carry

    lax.fori_loop(0, peers, one_peer, 0)


def received_records(recv, side, corner, cap):
    groups = side.shape[1]
    n_side = side.shape[2]
    n_corner = corner.shape[2]

    def one_peer(p, carry):
        for grp in range(groups):
            block = recv[p, :, grp * LANES : (grp + 1) * LANES].astype(F32)
            for k in range(cap):
                side[p * cap + k, grp] = block[k * n_side : (k + 1) * n_side]
                first = cap * n_side + k * n_corner
                corner[p * cap + k, grp] = block[first : first + n_corner]
        return carry

    lax.fori_loop(0, recv.shape[0], one_peer, 0)


def place_rim(padded, side, corner, side_sources, corner_sources, slot, zero_at, edge):
    for e in range(4):
        code = side_sources[slot, e]
        at = jnp.where(code < 0, zero_at, code)
        for grp in range(side.shape[1]):
            for c in range(RIM):
                piece = side[at, grp, c * edge : (c + 1) * edge]
                if e < 2:
                    row = c if e == 0 else RIM + edge + c
                    padded[grp, row, COL0 : COL0 + edge] = piece
                else:
                    col = COL0 - RIM + c if e == 2 else COL0 + edge + c
                    padded[grp, RIM : RIM + edge, col] = piece
        code = corner_sources[slot, e]
        at = jnp.where(code < 0, zero_at, code)
        row0 = RIM + edge if e // 2 else 0
        col0 = COL0 + edge if e % 2 else COL0 - RIM
        for grp in range(side.shape[1]):
            for r in range(RIM):
                padded[grp, row0 + r, col0 : col0 + RIM] = corner[
                    at, grp, RIM * r : RIM * r + RIM
                ]


def spread_taps(taps, kernel_ref):
    for grp in range(taps.shape[0]):
        for t in range(TAPS):
            row = kernel_ref[t : t + 1, grp * LANES : (grp + 1) * LANES].astype(F32)
            taps[grp, t] = jnp.broadcast_to(row, taps.shape[2:])


def conv_group(padded, taps, grp, edge, part, flipped, emit):
    blocks = edge // 8
    lane = lax.broadcasted_iota(jnp.int32, (8, LANES), 0)
    for blk in range(blocks):
        acc = [None] * edge
        for b in range(KERNEL):
            west = part == "rim" and blk == 0 and b < RIM
            east = part == "rim" and blk == blocks - 1 and b > RIM
            weights = []
            for a in range(KERNEL):
                t = a * KERNEL + b
                weights.append(taps[grp, TAPS - 1 - t if flipped else t])
            for r in range(edge + 2 * RIM):
                inner = RIM <= r < RIM + edge
                if part == "own" and not inner:
                    continue
                if part == "rim" and inner and not (west or east):
                    continue
                first = COL0 - RIM + b + 8 * blk
                cells = padded[grp, r, first : first + 8]
                if part == "rim" and inner:
                    keep = lane < RIM - b if west else lane >= 8 + RIM - b
                    cells = jnp.where(keep, cells, 0.0)
                for a in range(KERNEL):
                    row = r - a
                    if 0 <= row < edge:
                        term = cells * weights[a]
                        acc[row] = term if acc[row] is None else acc[row] + term
        for row in range(edge):
            emit(blk, row, acc[row])


def kernel_grad_group(padded, grad, sums, grp, edge):
    for b in range(KERNEL):
        acc = [None] * KERNEL
        for blk in range(edge // 8):
            rows = [grad[grp, RIM + i, COL0 + 8 * blk : COL0 + 8 * blk + 8] for i in range(edge)]
            for r in range(edge + 2 * RIM):
                first = COL0 - RIM + b + 8 * blk
                cells = padded[0, grp, r, first : first + 8]
                for a in range(KERNEL):
                    if 0 <= r - a < edge:
                        term = rows[r - a] * cells
                        acc[a] = term if acc[a] is None else acc[a] + term
        for a in range(KERNEL):
            sums[grp, a * KERNEL + b] += acc[a]


def pack_body(slot_ref, side_sends, corner_sends, field, send, cells, side, corner, *, edge):
    slots = field.shape[0]
    own = 4 * slots
    area = edge * edge
    for s in range(slots):
        factor = live_factor(slot_ref, s)
        for grp in range(cells.shape[0]):
            for i in list(range(edge)):
                row = field[s, i, :, grp * LANES : (grp + 1) * LANES].astype(F32)
                first = s * area + i * edge
                cells[grp, first : first + edge] = row * factor
    side[own] = jnp.zeros(side.shape[1:], F32)
    corner[...] = jnp.zeros_like(corner)
    own_records(cells, side, corner, 0, edge, slots)
    send_records(send, side, corner, side_sends, corner_sends, own)


def own_body(slot_ref, field, kernel_ref, mixed, padded, taps, *, edge):
    s = pl.program_id(0)
    groups = padded.shape[0]

    @pl.when(s == 0)
    def _():
        padded[...] = jnp.zeros_like(padded)
        spread_taps(taps, kernel_ref)

    factor = live_factor(slot_ref, s)
    for grp in range(groups):
        for i in range(edge):
            row = field[0, i, :, grp * LANES : (grp + 1) * LANES].astype(F32)
            padded[grp, RIM + i, COL0 : COL0 + edge] = row * factor

    def one_group(grp, carry):
        def emit(blk, row, total):
            mixed[0, grp, row, 8 * blk : 8 * blk + 8] = total

        conv_group(padded, taps, grp, edge, "own", False, emit)
        return carry

    lax.fori_loop(0, groups, one_group, 0)


def mlp_body(
    slot_ref,
    side_sources,
    corner_sources,
    side_sends,
    corner_sends,
    recv,
    field,
    mixed_own,
    cotangent,
    kernel_ref,
    expand,
    reduce,
    out,
    padded_out,
    grad_out,
    weights_out,
    send,
    side,
    corner,
    cells,
    taps,
    mixed,
    unit_ref,
    reduce_sum,
    expand_sum,
    *,
    edge,
    cap,
):
    s = pl.program_id(0)
    slots = pl.num_programs(0)
    groups = taps.shape[0]
    area = edge * edge
    n_slots = field.shape[0]
    base = recv.shape[0] * cap
    zero_at = base + 4 * n_slots
    hidden = expand.shape[1]
    channels = groups * LANES

    @pl.when(s == 0)
    def _():
        for t in range(n_slots):
            factor = live_factor(slot_ref, t)
            for grp in range(groups):
                for i in range(edge):
                    row = field[t, i, :, grp * LANES : (grp + 1) * LANES].astype(F32)
                    first = t * area + i * edge
                    cells[grp, first : first + edge] = row * factor
        side[zero_at] = jnp.zeros(side.shape[1:], F32)
        corner[...] = jnp.zeros_like(corner)
        received_records(recv, side, corner, cap)
        own_records(cells, side, corner, base, edge, n_slots)
        spread_taps(taps, kernel_ref)
        reduce_sum[...] = jnp.zeros_like(reduce_sum)
        expand_sum[...] = jnp.zeros_like(expand_sum)

    padded = padded_out.at[0]
    for grp in range(groups):
        for i in range(edge):
            first = pl.multiple_of(s * area + i * edge, 8)
            padded[grp, RIM + i, COL0 : COL0 + edge] = cells[grp, pl.ds(first, edge)]
    place_rim(padded, side, corner, side_sources, corner_sources, s, zero_at, edge)

    def one_group(grp, carry):
        def emit(blk, row, total):
            own = mixed_own[0, grp, row, 8 * blk : 8 * blk + 8]
            first = row * edge + 8 * blk
            mixed[grp, first : first + 8] = own if total is None else own + total

        conv_group(padded, taps, grp, edge, "rim", False, emit)
        return carry

    lax.fori_loop(0, groups, one_group, 0)

    factor = live_factor(slot_ref, s)
    parts = [mixed[grp] for grp in range(groups)]
    mean = sum(jnp.sum(part, axis=1, keepdims=True) for part in parts) * (1.0 / channels)
    parts = [part - mean for part in parts]
    var = sum(jnp.sum(part * part, axis=1, keepdims=True) for part in parts) * (1.0 / channels)
    scale = lax.rsqrt(var + LN_EPS)
    unit = jnp.concatenate([part * scale for part in parts], axis=1)
    unit_ref[...] = unit
    normed = unit.astype(BF16)
    cot = (cotangent[...].astype(F32) * factor).astype(BF16)
    update = None
    grad_norm = None
    for n in range(0, hidden, 256):
        pre = mxu(normed, expand[:, n : n + 256], 1, 0)
        act, slope = gelu_parts(pre)
        act = act.astype(BF16)
        grad_act = mxu(cot, reduce[n : n + 256], 1, 1)
        grad_pre = (grad_act * slope).astype(BF16)
        term = mxu(act, reduce[n : n + 256], 1, 0)
        update = term if update is None else update + term
        reduce_sum[:, n : n + 256] += mxu(cot, act, 0, 0)
        expand_sum[n // 256] += mxu(normed, grad_pre, 0, 0)
        term = mxu(grad_pre, expand[:, n : n + 256], 1, 1)
        grad_norm = term if grad_norm is None else grad_norm + term
    at = pl.ds(pl.multiple_of(s * area, 8), area)
    for grp in range(groups):
        lanes = slice(grp * LANES, (grp + 1) * LANES)
        out[:, lanes] = ((cells[grp, at] + update[:, lanes]) * factor).astype(BF16)

    unit = unit_ref[...]
    mean = jnp.sum(grad_norm, axis=1, keepdims=True) * (1.0 / channels)
    along = jnp.sum(grad_norm * unit, axis=1, keepdims=True) * (1.0 / channels)
    grad = (scale * (grad_norm - mean - unit * along)).astype(BF16)
    grad_out[...] = grad
    for grp in range(groups):
        cells[grp, at] = grad[:, grp * LANES : (grp + 1) * LANES].astype(F32)

    @pl.when(s == slots - 1)
    def _():
        weights_out[:hidden] = jnp.transpose(reduce_sum[...]).astype(BF16)
        for n in range(hidden // 256):
            first = hidden + n * channels
            weights_out[first : first + channels] = expand_sum[n].astype(BF16)
        own_records(cells, side, corner, base, edge, n_slots)
        send_records(send, side, corner, side_sends, corner_sends, zero_at, base)


def fill_padded(padded, grad_ref, edge):
    for grp in range(padded.shape[0]):
        for i in range(edge):
            row = grad_ref[i * edge : (i + 1) * edge, grp * LANES : (grp + 1) * LANES]
            padded[grp, RIM + i, COL0 : COL0 + edge] = row.astype(F32)


def kernel_grad_body(padded_field, grad_ref, kernel_out, padded, sums, *, edge):
    s = pl.program_id(0)
    groups = padded.shape[0]

    @pl.when(s == 0)
    def _():
        sums[...] = jnp.zeros_like(sums)

    fill_padded(padded, grad_ref, edge)

    def one_group(grp, carry):
        kernel_grad_group(padded_field, padded, sums, grp, edge)
        return carry

    lax.fori_loop(0, groups, one_group, 0)

    @pl.when(s == pl.num_programs(0) - 1)
    def _():
        kernel_out[...] = jnp.zeros_like(kernel_out)
        for grp in range(groups):
            lanes = slice(grp * LANES, (grp + 1) * LANES)
            kernel_out[:TAPS, lanes] = jnp.sum(sums[grp], axis=1)


def final_body(
    slot_ref,
    side_sources,
    corner_sources,
    recv,
    grad_ref,
    cotangent,
    kernel_ref,
    *rest,
    edge,
    cap,
    first_slot,
):
    out, cells_out, side, corner, cells, padded, taps = rest[-7:]
    step = pl.program_id(0)
    s = step + first_slot
    groups = taps.shape[0]
    area = edge * edge
    n_slots = grad_ref.shape[0] // area
    base = recv.shape[0] * cap
    zero_at = base + 4 * n_slots

    @pl.when(step == 0)
    def _():
        for grp in range(groups):
            cells[grp] = grad_ref[:, grp * LANES : (grp + 1) * LANES].astype(F32)
        side[zero_at] = jnp.zeros(side.shape[1:], F32)
        corner[zero_at] = jnp.zeros(corner.shape[1:], F32)
        received_records(recv, side, corner, cap)
        own_records(cells, side, corner, base, edge, n_slots)
        spread_taps(taps, kernel_ref)

    for grp in range(groups):
        for i in range(edge):
            first = pl.multiple_of(s * area + i * edge, 8)
            padded[grp, RIM + i, COL0 : COL0 + edge] = cells[grp, pl.ds(first, edge)]
    place_rim(padded, side, corner, side_sources, corner_sources, s, zero_at, edge)
    factor = live_factor(slot_ref, s)

    def one_group(grp, carry):
        def emit(blk, row, total):
            first = row * edge + 8 * blk
            cells_out[grp, first : first + 8] = total

        conv_group(padded, taps, grp, edge, "all", True, emit)
        return carry

    lax.fori_loop(0, groups, one_group, 0)
    for grp in range(groups):
        lanes = slice(grp * LANES, (grp + 1) * LANES)
        total = cotangent[:, lanes].astype(F32) + cells_out[grp]
        out[:, lanes] = (total * factor).astype(BF16)


def weights_body(order, *refs, hidden, factor):
    blocks, (kernel_out, expand_out, reduce_out, rows) = refs[:-4], refs[-4:]
    channels = reduce_out.shape[1]
    part = 2 * hidden // len(blocks)
    kernel_sum = None
    for at, block in enumerate(blocks):
        first = pl.multiple_of(order[at] * part, 8)
        rows[pl.ds(first, part)] = block[:part].astype(F32) * factor
        kernel = block[part:].astype(F32)
        kernel_sum = kernel if kernel_sum is None else kernel_sum + kernel
    kernel_out[...] = kernel_sum[:TAPS] * factor
    reduce_out[...] = rows[:hidden]
    for n in range(hidden // 256):
        first = hidden + n * channels
        expand_out[:, n * 256 : (n + 1) * 256] = rows[first : first + channels]


def call(body, grid, ins, outs, scratch, flops=0, moved=0, aliases=None):
    in_specs = []
    for array, block, index in ins:
        if block is None:
            in_specs.append(pl.BlockSpec(memory_space=index or pltpu.SMEM))
        else:
            in_specs.append(pl.BlockSpec(block, index))
    return pl.pallas_call(
        body,
        grid=grid,
        in_specs=in_specs,
        out_specs=[pl.BlockSpec(block, index) for _, _, block, index in outs],
        out_shape=[jax.ShapeDtypeStruct(shape, dtype) for shape, dtype, _, _ in outs],
        scratch_shapes=scratch,
        input_output_aliases=aliases or {},
        compiler_params=pltpu.CompilerParams(vmem_limit_bytes=VMEM_LIMIT),
        cost_estimate=pl.CostEstimate(flops=flops, bytes_accessed=moved, transcendentals=0),
    )(*[array for array, _, _ in ins])


def whole(array):
    rank = array.ndim
    return (array, array.shape, lambda s: (0,) * rank)


def swap(blocks, axis):
    return lax.all_to_all(blocks, axis, split_axis=0, concat_axis=0, tiled=True)


def spread_blocks(blocks, axis):
    size = blocks.shape[0]
    me = lax.axis_index(axis)
    take = lambda at: lax.dynamic_index_in_dim(blocks, at, 0, keepdims=False)
    parts = [take(me)]
    for step in range(1, size):
        perm = [(i, (i + step) % size) for i in range(size)]
        parts.append(lax.ppermute(take((me + step) % size), axis, perm))
    return parts


def gather_blocks(block, axis):
    size = lax.axis_size(axis)
    me = lax.axis_index(axis)
    swap_pair = [(i, i ^ 1) for i in range(size)]
    parts = [block]
    order = [me]
    for step in range(2, size, 2):
        perm = [(i, (i + step) % size) for i in range(size)]
        parts.append(lax.ppermute(block, axis, perm))
        order.append((me - step) % size)
    passed = [lax.ppermute(part, axis, swap_pair) for part in parts]
    partner = me ^ 1
    order += [partner] + [(partner - step) % size for step in range(2, size, 2)]
    return parts + passed, jnp.stack(order).astype(jnp.int32)


def on_device(
    ocean_fields,
    slot_tiles,
    side_sources,
    corner_sources,
    side_sends,
    corner_sends,
    depth_kernel,
    expand_weight,
    reduce_weight,
    field_cotangent,
):
    slots, edge, _, channels = ocean_fields.shape
    hidden = expand_weight.shape[1]
    tiles = lax.axis_size("tile")
    basins = lax.axis_size("basin")
    cap = side_sends.shape[2]
    groups = channels // LANES
    area = edge * edge
    cells = slots * area
    n_side = RIM * edge
    n_corner = 16
    send_rows = cap * (n_side + n_corner)
    table = tiles * cap + 4 * slots + 1
    wide = edge + 2 * COL0
    tall = edge + 2 * RIM

    cot_rows = field_cotangent.reshape(cells, channels)
    scalar = lambda array: (array, None, None)
    by_slot = lambda array, width: (array, (area, width), lambda s: (s, 0))
    taps = pltpu.VMEM((groups, TAPS, 8, LANES), F32)
    cell_scratch = pltpu.VMEM((groups, cells, LANES), F32)
    padded_scratch = pltpu.VMEM((groups, tall, wide, LANES), F32)
    own_side = pltpu.VMEM((4 * slots + 1, groups, n_side, LANES), F32)
    own_corner = pltpu.VMEM((4 * slots + 1, groups, n_corner, LANES), F32)
    all_side = pltpu.VMEM((table, groups, n_side, LANES), F32)
    all_corner = pltpu.VMEM((table, groups, n_corner, LANES), F32)
    send_out = ((tiles, send_rows, channels), BF16, (tiles, send_rows, channels), lambda s: (0, 0, 0))
    tile_block = (1, groups, edge, edge, LANES)
    tile_out = ((slots,) + tile_block[1:], F32, tile_block, lambda s: (s, 0, 0, 0, 0))
    kernel_rows = tiles * 8 * -(-TAPS // (8 * tiles))
    mlp_flops = 6 * cells * channels * hidden
    field_bytes = cells * channels * 4

    (send,) = call(
        functools.partial(pack_body, edge=edge),
        (1,),
        [scalar(slot_tiles), scalar(side_sends), scalar(corner_sends), whole(ocean_fields)],
        [send_out],
        [cell_scratch, own_side, own_corner],
        moved=field_bytes,
    )
    recv = swap(send, "tile")
    (mixed_own,) = call(
        functools.partial(own_body, edge=edge),
        (slots,),
        [
            scalar(slot_tiles),
            (ocean_fields, (1, edge, edge, channels), lambda s: (s, 0, 0, 0)),
            whole(depth_kernel),
        ],
        [tile_out],
        [padded_scratch, taps],
        flops=mlp_flops,
        moved=2 * field_bytes,
    )
    next_rows, padded, grad_rows, weights, send = call(
        functools.partial(mlp_body, edge=edge, cap=cap),
        (slots,),
        [
            scalar(slot_tiles),
            scalar(side_sources),
            scalar(corner_sources),
            scalar(side_sends),
            scalar(corner_sends),
            whole(recv),
            whole(ocean_fields),
            (mixed_own, tile_block, lambda s: (s, 0, 0, 0, 0)),
            by_slot(cot_rows, channels),
            whole(depth_kernel),
            whole(expand_weight),
            whole(reduce_weight),
        ],
        [
            ((cells, channels), BF16, (area, channels), lambda s: (s, 0)),
            (
                (slots, groups, tall, wide, LANES),
                F32,
                (1, groups, tall, wide, LANES),
                lambda s: (s, 0, 0, 0, 0),
            ),
            ((cells, channels), BF16, (area, channels), lambda s: (s, 0)),
            ((2 * hidden, channels), BF16, (2 * hidden, channels), lambda s: (0, 0)),
            send_out,
        ],
        [
            all_side,
            all_corner,
            cell_scratch,
            taps,
            pltpu.VMEM((groups, area, LANES), F32),
            pltpu.VMEM((area, channels), F32),
            pltpu.VMEM((channels, hidden), F32),
            pltpu.VMEM((hidden // 256, channels, 256), F32),
        ],
        flops=2 * mlp_flops,
        moved=6 * field_bytes,
    )
    recv = swap(send, "tile")
    rows = 2 * hidden
    blocks = spread_blocks(weights.reshape(basins, rows // basins, channels), "basin")
    (kernel_part,) = call(
        functools.partial(kernel_grad_body, edge=edge),
        (slots,),
        [
            (padded, (1, groups, tall, wide, LANES), lambda s: (s, 0, 0, 0, 0)),
            by_slot(grad_rows, channels),
        ],
        [((kernel_rows, channels), F32, (kernel_rows, channels), lambda s: (0, 0))],
        [padded_scratch, taps],
        flops=mlp_flops,
        moved=4 * field_bytes,
    )
    mine = sum(block.astype(F32) for block in blocks).astype(BF16)
    part = rows // basins // tiles
    mine = jnp.concatenate(
        [
            mine.reshape(tiles, part, channels),
            kernel_part.astype(BF16).reshape(tiles, kernel_rows // tiles, channels),
        ],
        axis=1,
    )
    blocks = swap(mine, "tile")
    half = slots // 2

    def final(first_slot, count, previous):
        rows_at = lambda s: (s + first_slot, 0)
        ins = [
            scalar(slot_tiles),
            scalar(side_sources),
            scalar(corner_sources),
            whole(recv),
            whole(grad_rows),
            (cot_rows, (area, channels), rows_at),
            whole(depth_kernel),
        ]
        if previous is not None:
            ins.append((previous, None, pl.ANY))
        (rows_out,) = call(
            functools.partial(final_body, edge=edge, cap=cap, first_slot=first_slot),
            (count,),
            ins,
            [((cells, channels), BF16, (area, channels), rows_at)],
            [
                pltpu.VMEM((groups, area, LANES), F32),
                all_side,
                all_corner,
                cell_scratch,
                padded_scratch,
                taps,
            ],
            flops=mlp_flops // 2,
            moved=3 * field_bytes,
            aliases=None if previous is None else {len(ins) - 1: 0},
        )
        return rows_out

    grad_field = final(0, half, None)
    mine = jnp.sum(blocks.astype(F32), axis=0).astype(BF16)
    blocks = swap(jnp.broadcast_to(mine[None], (tiles,) + mine.shape), "tile")
    mine = jnp.concatenate(
        [
            blocks[:, :part].reshape(rows // basins, channels),
            blocks[:, part:].reshape(kernel_rows, channels),
        ],
        axis=0,
    )
    blocks, order = gather_blocks(mine, "basin")
    grad_field = final(half, slots - half, grad_field)
    factor = 1.0 / math.sqrt(basins * tiles * cells)
    kernel_total, expand_total, reduce_total = call(
        functools.partial(weights_body, hidden=hidden, factor=factor),
        (1,),
        [scalar(order)] + [whole(block) for block in blocks],
        [
            ((TAPS, channels), F32, (TAPS, channels), lambda s: (0, 0)),
            ((channels, hidden), F32, (channels, hidden), lambda s: (0, 0)),
            ((hidden, channels), F32, (hidden, channels), lambda s: (0, 0)),
        ],
        [pltpu.VMEM((rows, channels), F32)],
        moved=6 * hidden * channels * 2,
    )
    shape = ocean_fields.shape
    return (
        next_rows.reshape(shape),
        grad_field.reshape(shape),
        kernel_total,
        expand_total,
        reduce_total,
    )


def solution(mesh):
    split = ("basin", "tile")
    field = P(split, None, None, None)
    table = P(split, None, None)
    pair = P(split, None)

    return jax.shard_map(
        on_device,
        mesh=mesh,
        in_specs=(field, P(split), pair, pair, table, table, P(), P(), P(), field),
        out_specs=(field, field, P(), P(), P()),
        check_vma=False,
    )
```

profile of v0, /device:TPU:0, one launch (start us, length us, event | category | flops | bytes accessed | tf_op | source)
XLA Modules:
  0.0 144.1 jit_solution(12964723161879778888)
XLA Ops:
  0.6 1.3 copy.18.side_sends
  2.0 1.3 copy.19.corner_sends
  3.3 2.6 %shard_map.137 = bf16[8,176,256]{2,1,0:T(8,128)(2,1)} custom-call(s32[4]{0:T(128)} %slot_ref.9, s32[1,8,2]{2,1,0:T(8,128)} %copy.18.side_sends, s32[1,8,2]{2,1,0:T(8,128)} %copy.19.corner_sends, bf16[4,24,24,256]{3,2,1,0:T(8,128)(2,1)} %field.5), custom_call_target="tpu_custom_call" | custom-call | bytes 2359296 | tf_op jit(solution)/shard_map/pallas_call | solution.py:449
  5.9 7.3 %all-to-all-start = ((bf16[8,176,256]{2,1,0:T(8,128)(2,1)}), bf16[8,176,256]{2,1,0:T(8,128)(2,1)S(1)}, u32[]{:S(2)}, u32[]{:S(2)}) async-start(bf16[8,176,256]{2,1,0:T(8,128)(2,1)} %shard_map.137), calls=%async_computation | async-start | bytes 1441792 | tf_op jit(solution)/shard_map/all_to_all | solution.py:468
  13.2 12.2 %shard_map.138.mixed_own = f32[4,2,24,24,128]{4,3,2,1,0:T(8,128)} custom-call(s32[4]{0:T(128)} %slot_ref.9, bf16[4,24,24,256]{3,2,1,0:T(8,128)(2,1)} %field.5, bf16[49,256]{1,0:T(8,128)(2,1)} %kernel_ref.7), custom_call_target="tpu_custom_call" | custom-call | flops 3623878656 | bytes 4718592 | tf_op jit(solution)/shard_map/pallas_call | solution.py:449
  25.5 6.5 %all-to-all-done.recv = bf16[8,176,256]{2,1,0:T(8,128)(2,1)S(1)} async-done(((bf16[8,176,256]{2,1,0:T(8,128)(2,1)}), bf16[8,176,256]{2,1,0:T(8,128)(2,1)S(1)}, u32[]{:S(2)}, u32[]{:S(2)}) %all-to-all-start) | async-done | bytes 720928 | tf_op jit(solution)/shard_map/all_to_all | solution.py:468
  32.0 0.0 copy-start.1
  32.0 0.9 copy-done.1
  32.8 21.1 %shard_map.139 = (bf16[2304,256]{1,0:T(8,128)(2,1)}, f32[4,2,30,40,128]{4,3,2,1,0:T(8,128)}, bf16[2304,256]{1,0:T(8,128)(2,1)}, bf16[2048,256]{1,0:T(8,128)(2,1)}, bf16[8,176,256]{2,1,0:T(8,128)(2,1)}) custom-call(s32[4]{0:T(128)} %slot_ref.9, s32[4,4]{1,0:T(4,128)} %side_sources.5, s32[4,4]{1,0:T(4,128)} %corner_sources.5, s32[1,8,2]{2,1,0:T(8,128)} %copy.18.side_sends, ...), custom_call_target="tpu_custom_call" | custom-call | flops 7247757312 | bytes 14155776 | tf_op jit(solution)/shard_map/pallas_call | solution.py:449
  53.9 1.2 dynamic-slice_bitcast_fusion.2
  55.1 0.1 collective-permute-start.2
  55.1 1.6 %collective-permute-start.1 = (bf16[512,256]{1,0:T(8,128)(2,1)S(1)}, bf16[512,256]{1,0:T(8,128)(2,1)S(1)}, u32[]{:S(2)}, u32[]{:S(2)}) collective-permute-start(bf16[512,256]{1,0:T(8,128)(2,1)S(1)} %get-tuple-element.23), channel_id=1, source_target_pairs={{0,16},{8,24},{16,0},{24,8},{1,17},{9,25},{17,1},{25,9},{2,18},{10... | collective-permute-start | bytes 786440 | tf_op jit(solution)/shard_map/ppermute | solution.py:478
  56.7 0.2 collective-permute-start
  56.8 13.5 %shard_map.142 = f32[64,256]{1,0:T(8,128)} custom-call(f32[4,2,30,40,128]{4,3,2,1,0:T(8,128)} %get-tuple-element.17.padded_field, bf16[2304,256]{1,0:T(8,128)(2,1)} %get-tuple-element.15.grad_ref), custom_call_target="tpu_custom_call" | custom-call | flops 3623878656 | bytes 9437184 | tf_op jit(solution)/shard_map/pallas_call | solution.py:449
  70.4 0.8 convert_bitcast_fusion
  71.2 0.0 collective-permute-done.2
  71.2 0.0 collective-permute-done.1
  71.2 0.0 collective-permute-done
  71.2 1.1 fusion.2
  72.3 14.8 %all_to_all.20 = bf16[8,72,256]{2,1,0:T(8,128)(2,1)S(1)} all-to-all(bf16[8,72,256]{2,1,0:T(8,128)(2,1)S(1)} %pad_maximum_fusion), channel_id=1, replica_groups=mesh['basin'=4,'tile'=8] {'tile'}, dimensions={0} | all-to-all | bytes 589824 | tf_op jit(solution)/shard_map/all_to_all | solution.py:468
  87.2 13.7 %all_to_all.21 = bf16[8,72,256]{2,1,0:T(8,128)(2,1)S(1)} all-to-all(bf16[8,72,256]{2,1,0:T(8,128)(2,1)S(1)} %broadcast_in_dim.2), channel_id=1, replica_groups=mesh['basin'=4,'tile'=8] {'tile'}, dimensions={0} | all-to-all | bytes 589824 | tf_op jit(solution)/shard_map/all_to_all | solution.py:468
  100.8 3.7 %all-to-all-start.1 = ((bf16[8,176,256]{2,1,0:T(8,128)(2,1)}), bf16[8,176,256]{2,1,0:T(8,128)(2,1)S(1)}, u32[]{:S(2)}, u32[]{:S(2)}) async-start(bf16[8,176,256]{2,1,0:T(8,128)(2,1)} %get-tuple-element.14), calls=%async_computation.1 | async-start | bytes 1441792 | tf_op jit(solution)/shard_map/all_to_all | solution.py:468
  104.7 0.0 copy-start
  104.7 0.6 collective-permute-start.3
  105.3 0.7 pad_add_fusion.order
  105.9 0.0 collective-permute-start.4
  105.9 6.3 %collective-permute-done.3.refs_1_ = bf16[576,256]{1,0:T(8,128)(2,1)S(1)} collective-permute-done((bf16[576,256]{1,0:T(8,128)(2,1)S(1)}, bf16[576,256]{1,0:T(8,128)(2,1)S(1)}, u32[]{:S(2)}, u32[]{:S(2)}) %collective-permute-start.3) | collective-permute-done | bytes 294944 | tf_op jit(solution)/shard_map/ppermute | solution.py:490
  112.3 0.0 copy-start.3
  112.3 0.0 collective-permute-start.5
  112.3 10.1 %all-to-all-done.1.recv = bf16[8,176,256]{2,1,0:T(8,128)(2,1)S(1)} async-done(((bf16[8,176,256]{2,1,0:T(8,128)(2,1)}), bf16[8,176,256]{2,1,0:T(8,128)(2,1)S(1)}, u32[]{:S(2)}, u32[]{:S(2)}) %all-to-all-start.1) | async-done | bytes 720928 | tf_op jit(solution)/shard_map/all_to_all | solution.py:468
  122.4 0.0 copy-start.2
  122.4 0.9 copy-done.2
  123.3 8.3 %shard_map.140.rest_0_ = bf16[2304,256]{1,0:T(8,128)(2,1)} custom-call(s32[4]{0:T(128)} %slot_ref.9, s32[4,4]{1,0:T(4,128)} %side_sources.5, s32[4,4]{1,0:T(4,128)} %corner_sources.5, bf16[8,176,256]{2,1,0:T(8,128)(2,1)} %copy-done.2, bf16[2304,256]{1,0:T(8,128)(2,1)} %get-tuple-element.15.grad_ref, bf16[2304,256]{1,0:T(8,128)(2,1)} %bitcast.28, ...), custom_call_target="tpu_custom_call" | custom-call | flops 1811939328 | bytes 7077888 | tf_op jit(solution)/shard_map/pallas_call | solution.py:449
  131.5 0.0 copy-done
  131.5 8.3 %shard_map.141 = bf16[2304,256]{1,0:T(8,128)(2,1)} custom-call(s32[4]{0:T(128)} %slot_ref.9, s32[4,4]{1,0:T(4,128)} %side_sources.5, s32[4,4]{1,0:T(4,128)} %corner_sources.5, bf16[8,176,256]{2,1,0:T(8,128)(2,1)} %copy-done.2, bf16[2304,256]{1,0:T(8,128)(2,1)} %get-tuple-element.15.grad_ref, ...), custom_call_target="tpu_custom_call", output_to_operand_aliasing={{}: (7, {})} | custom-call | flops 1811939328 | bytes 7077888 | tf_op jit(solution)/shard_map/pallas_call | solution.py:449
  139.8 0.0 copy-done.3
  139.8 0.0 collective-permute-done.4.refs_2_
  139.9 0.0 copy-start.4
  139.9 0.0 collective-permute-done.5.refs_3_
  139.9 0.7 copy-done.4
  140.6 0.0 copy-start.5
  140.6 0.7 copy-done.5
  141.3 2.8 %shard_map.143 = (f32[49,256]{1,0:T(8,128)}, f32[256,1024]{1,0:T(8,128)}, f32[1024,256]{1,0:T(8,128)}) custom-call(s32[4]{0:T(128)} %pad_add_fusion.order, bf16[576,256]{1,0:T(8,128)(2,1)} %copy-done, bf16[576,256]{1,0:T(8,128)(2,1)} %copy-done.3, bf16[576,256]{1,0:T(8,128)(2,1)} %copy-done.4, bf16[576,256]{1,0:T(8,128)(2,1)} %copy-done.5), custom_call_target="tpu_custom_call" | custom-call | bytes 3145728 | tf_op jit(solution)/shard_map/pallas_call | solution.py:449
  (6 shorter events, 0.1 us)
Async XLA Ops:
  5.9 26.0 %all-to-all-start = ((bf16[8,176,256]{2,1,0:T(8,128)(2,1)}), bf16[8,176,256]{2,1,0:T(8,128)(2,1)S(1)}, u32[]{:S(2)}, u32[]{:S(2)}) async-start(bf16[8,176,256]{2,1,0:T(8,128)(2,1)} %shard_map.137), calls=%async_computation | async-start | bytes 1441792 | tf_op jit(solution)/shard_map/all_to_all | solution.py:468
  32.0 0.9 copy-start.1
  55.1 16.1 %collective-permute-start.2 = (bf16[512,256]{1,0:T(8,128)(2,1)S(1)}, bf16[512,256]{1,0:T(8,128)(2,1)S(1)}, u32[]{:S(2)}, u32[]{:S(2)}) collective-permute-start(bf16[512,256]{1,0:T(8,128)(2,1)S(1)} %get-tuple-element.22), channel_id=1, source_target_pairs={{0,24},{8,0},{16,8},{24,16},{1,25},{9,1},{17,9},{25,17},{2,26},{10... | collective-permute-start | bytes 786440 | tf_op jit(solution)/shard_map/ppermute | solution.py:478
  55.1 16.1 %collective-permute-start.1 = (bf16[512,256]{1,0:T(8,128)(2,1)S(1)}, bf16[512,256]{1,0:T(8,128)(2,1)S(1)}, u32[]{:S(2)}, u32[]{:S(2)}) collective-permute-start(bf16[512,256]{1,0:T(8,128)(2,1)S(1)} %get-tuple-element.23), channel_id=1, source_target_pairs={{0,16},{8,24},{16,0},{24,8},{1,17},{9,25},{17,1},{25,9},{2,18},{10... | collective-permute-start | bytes 786440 | tf_op jit(solution)/shard_map/ppermute | solution.py:478
  56.7 14.5 %collective-permute-start = (bf16[512,256]{1,0:T(8,128)(2,1)S(1)}, bf16[512,256]{1,0:T(8,128)(2,1)S(1)}, u32[]{:S(2)}, u32[]{:S(2)}) collective-permute-start(bf16[512,256]{1,0:T(8,128)(2,1)S(1)} %get-tuple-element.21), channel_id=1, source_target_pairs={{0,8},{8,16},{16,24},{24,0},{1,9},{9,17},{17,25},{25,1},{2,10},{10... | collective-permute-start | bytes 786440 | tf_op jit(solution)/shard_map/ppermute | solution.py:478
  100.8 21.5 %all-to-all-start.1 = ((bf16[8,176,256]{2,1,0:T(8,128)(2,1)}), bf16[8,176,256]{2,1,0:T(8,128)(2,1)S(1)}, u32[]{:S(2)}, u32[]{:S(2)}) async-start(bf16[8,176,256]{2,1,0:T(8,128)(2,1)} %get-tuple-element.14), calls=%async_computation.1 | async-start | bytes 1441792 | tf_op jit(solution)/shard_map/all_to_all | solution.py:468
  104.7 26.9 %copy-start = (bf16[576,256]{1,0:T(8,128)(2,1)}, bf16[576,256]{1,0:T(8,128)(2,1)S(1)}, u32[]{:S(2)}) copy-start(bf16[576,256]{1,0:T(8,128)(2,1)S(1)} %pad_maximum_fusion.1.refs_0_) | copy-start | bytes 884740
  104.7 7.6 %collective-permute-start.3 = (bf16[576,256]{1,0:T(8,128)(2,1)S(1)}, bf16[576,256]{1,0:T(8,128)(2,1)S(1)}, u32[]{:S(2)}, u32[]{:S(2)}) collective-permute-start(bf16[576,256]{1,0:T(8,128)(2,1)S(1)} %pad_maximum_fusion.1.refs_0_), channel_id=1, source_target_pairs={{0,16},{8,24},{16,0},{24,8},{1,17},{9,25},{17,1},{25,9},{2,18},{10... | collective-permute-start | bytes 884744 | tf_op jit(solution)/shard_map/ppermute | solution.py:490
  105.9 33.9 %collective-permute-start.4 = (bf16[576,256]{1,0:T(8,128)(2,1)S(1)}, bf16[576,256]{1,0:T(8,128)(2,1)S(1)}, u32[]{:S(2)}, u32[]{:S(2)}) collective-permute-start(bf16[576,256]{1,0:T(8,128)(2,1)S(1)} %pad_maximum_fusion.1.refs_0_), channel_id=1, source_target_pairs={{0,8},{8,0},{16,24},{24,16},{1,9},{9,1},{17,25},{25,17},{2,10},{10... | collective-permute-start | bytes 884744 | tf_op jit(solution)/shard_map/ppermute | solution.py:492
  112.3 27.6 %copy-start.3 = (bf16[576,256]{1,0:T(8,128)(2,1)}, bf16[576,256]{1,0:T(8,128)(2,1)S(1)}, u32[]{:S(2)}) copy-start(bf16[576,256]{1,0:T(8,128)(2,1)S(1)} %collective-permute-done.3.refs_1_) | copy-start | bytes 884740
  112.3 27.6 %collective-permute-start.5 = (bf16[576,256]{1,0:T(8,128)(2,1)S(1)}, bf16[576,256]{1,0:T(8,128)(2,1)S(1)}, u32[]{:S(2)}, u32[]{:S(2)}) collective-permute-start(bf16[576,256]{1,0:T(8,128)(2,1)S(1)} %collective-permute-done.3.refs_1_), channel_id=1, source_target_pairs={{0,8},{8,0},{16,24},{24,16},{1,9},{9,1},{17,25},{25,17},{2,10},{10... | collective-permute-start | bytes 884744 | tf_op jit(solution)/shard_map/ppermute | solution.py:492
  122.4 0.9 copy-start.2
  139.9 0.7 copy-start.4
  140.6 0.7 copy-start.5
where the time goes:
time: 145 us; the launch traced here: 144 us
  Pallas kernels  68.9 us (48%)
  blocking collectives  28.4 us (20%)
  waiting for transfers between devices  23 us (16%)
  starting transfers between devices  13.4 us (9%)
  local copies, waits for them, and re-layouts  7.03 us (5%)
  other arithmetic  2.67 us (2%)
    pallas_call x7, Pallas kernels, call(): pl.pallas_call(body, grid=grid, in_specs=in_specs, out_specs=[pl.BlockSpe...  68.9 us
    all_to_all x2, blocking collectives, swap(): return lax.all_to_all(blocks, axis, split_axis=0, concat_axis=0, tiled=True)  28.4 us
    all_to_all x2, waiting for transfers between devices, swap(): return lax.all_to_all(blocks, axis, split_axis=0, concat_axis=0, tiled=True)  16.6 us
    all_to_all x2, starting transfers between devices, swap(): return lax.all_to_all(blocks, axis, split_axis=0, concat_axis=0, tiled=True)  11 us
    ppermute x1, waiting for transfers between devices, gather_blocks(): parts.append(lax.ppermute(block, axis, perm))  6.33 us
    unnamed x14, local copies, waits for them, and re-layouts  5.82 us
  transfers between devices with their start and end apart: 8, of which 3 were waited for; matrix products, arithmetic and copies ran while one was open for 1% of the time, Pallas kernels for 29%

commit v1 on v0

--- a/solution.py
+++ b/solution.py
@@ -61,14 +61,14 @@
 def send_records(send, side, corner, side_sends, corner_sends, zero_at, base=0):
     peers = send.shape[0]
     groups = side.shape[1]
-    cap = side_sends.shape[2]
+    cap = side_sends.shape[0]
 
     def one_peer(p, carry):
         for grp in range(groups):
             pieces = []
             for table, sends in ((side, side_sends), (corner, corner_sends)):
                 for k in range(cap):
-                    code = sends[0, p, k]
+                    code = sends[k, p]
                     pieces.append(table[jnp.where(code < 0, zero_at, code + base), grp])
             block = jnp.concatenate(pieces, axis=0)
             send[p, :, grp * LANES : (grp + 1) * LANES] = block.astype(BF16)
@@ -190,9 +190,12 @@
     send_records(send, side, corner, side_sends, corner_sends, own)
 
 
-def own_body(slot_ref, field, kernel_ref, mixed, padded, taps, *, edge):
+def own_body(
+    slot_ref, field, kernel_ref, cotangent, reduce, mixed, grad_act, padded, taps, *, edge
+):
     s = pl.program_id(0)
     groups = padded.shape[0]
+    share = cotangent.shape[0] // groups
 
     @pl.when(s == 0)
     def _():
@@ -209,6 +212,10 @@
         def emit(blk, row, total):
             mixed[0, grp, row, 8 * blk : 8 * blk + 8] = total
 
+        rows = pl.ds(pl.multiple_of(grp * share, 16), share)
+        cot = (cotangent[rows].astype(F32) * factor).astype(BF16)
+        for n in range(0, reduce.shape[0], 256):
+            grad_act[rows, n : n + 256] = mxu(cot, reduce[n : n + 256], 1, 1)
         conv_group(padded, taps, grp, edge, "own", False, emit)
         return carry
 
@@ -224,6 +231,7 @@
     recv,
     field,
     mixed_own,
+    grad_act_ref,
     cotangent,
     kernel_ref,
     expand,
@@ -306,8 +314,7 @@
         pre = mxu(normed, expand[:, n : n + 256], 1, 0)
         act, slope = gelu_parts(pre)
         act = act.astype(BF16)
-        grad_act = mxu(cot, reduce[n : n + 256], 1, 1)
-        grad_pre = (grad_act * slope).astype(BF16)
+        grad_pre = (grad_act_ref[:, n : n + 256] * slope).astype(BF16)
         term = mxu(act, reduce[n : n + 256], 1, 0)
         update = term if update is None else update + term
         reduce_sum[:, n : n + 256] += mxu(cot, act, 0, 0)
@@ -362,10 +369,11 @@
 
     @pl.when(s == pl.num_programs(0) - 1)
     def _():
-        kernel_out[...] = jnp.zeros_like(kernel_out)
         for grp in range(groups):
             lanes = slice(grp * LANES, (grp + 1) * LANES)
-            kernel_out[:TAPS, lanes] = jnp.sum(sums[grp], axis=1)
+            rows = jnp.sum(sums[grp], axis=1)
+            empty = jnp.zeros((kernel_out.shape[0] - TAPS, LANES), F32)
+            kernel_out[:, lanes] = jnp.concatenate([rows, empty], axis=0).astype(BF16)
 
 
 def final_body(
@@ -422,13 +430,16 @@
         out[:, lanes] = (total * factor).astype(BF16)
 
 
-def weights_body(order, *refs, hidden, factor):
+def weights_body(device, *refs, hidden, factor):
     blocks, (kernel_out, expand_out, reduce_out, rows) = refs[:-4], refs[-4:]
     channels = reduce_out.shape[1]
     part = 2 * hidden // len(blocks)
     kernel_sum = None
     for at, block in enumerate(blocks):
-        first = pl.multiple_of(order[at] * part, 8)
+        pairs = len(blocks) // 2
+        holder = device[0] if at < pairs else device[0] ^ 1
+        source = lax.rem(holder - 2 * (at % pairs) + len(blocks), len(blocks))
+        first = pl.multiple_of(source * part, 8)
         rows[pl.ds(first, part)] = block[:part].astype(F32) * factor
         kernel = block[part:].astype(F32)
         kernel_sum = kernel if kernel_sum is None else kernel_sum + kernel
@@ -439,11 +450,11 @@
         expand_out[:, n * 256 : (n + 1) * 256] = rows[first : first + channels]
 
 
-def call(body, grid, ins, outs, scratch, flops=0, moved=0, aliases=None):
+def call(body, grid, ins, outs, scratch, flops=0, moved=0, aliases=None, limit=VMEM_LIMIT):
     in_specs = []
     for array, block, index in ins:
         if block is None:
-            in_specs.append(pl.BlockSpec(memory_space=index or pltpu.SMEM))
+            in_specs.append(pl.BlockSpec(memory_space=index))
         else:
             in_specs.append(pl.BlockSpec(block, index))
     return pl.pallas_call(
@@ -454,7 +465,7 @@
         out_shape=[jax.ShapeDtypeStruct(shape, dtype) for shape, dtype, _, _ in outs],
         scratch_shapes=scratch,
         input_output_aliases=aliases or {},
-        compiler_params=pltpu.CompilerParams(vmem_limit_bytes=VMEM_LIMIT),
+        compiler_params=pltpu.CompilerParams(vmem_limit_bytes=limit),
         cost_estimate=pl.CostEstimate(flops=flops, bytes_accessed=moved, transcendentals=0),
     )(*[array for array, _, _ in ins])
 
@@ -481,18 +492,13 @@
 
 def gather_blocks(block, axis):
     size = lax.axis_size(axis)
-    me = lax.axis_index(axis)
     swap_pair = [(i, i ^ 1) for i in range(size)]
     parts = [block]
-    order = [me]
     for step in range(2, size, 2):
         perm = [(i, (i + step) % size) for i in range(size)]
         parts.append(lax.ppermute(block, axis, perm))
-        order.append((me - step) % size)
     passed = [lax.ppermute(part, axis, swap_pair) for part in parts]
-    partner = me ^ 1
-    order += [partner] + [(partner - step) % size for step in range(2, size, 2)]
-    return parts + passed, jnp.stack(order).astype(jnp.int32)
+    return parts + passed
 
 
 def on_device(
@@ -523,7 +529,10 @@
     tall = edge + 2 * RIM
 
     cot_rows = field_cotangent.reshape(cells, channels)
-    scalar = lambda array: (array, None, None)
+    side_sends = jnp.transpose(side_sends.reshape(tiles, cap))
+    corner_sends = jnp.transpose(corner_sends.reshape(tiles, cap))
+    scalar = lambda array: (array, None, pltpu.SMEM)
+    placed = lambda array: (array, None, pltpu.VMEM)
     by_slot = lambda array, width: (array, (area, width), lambda s: (s, 0))
     taps = pltpu.VMEM((groups, TAPS, 8, LANES), F32)
     cell_scratch = pltpu.VMEM((groups, cells, LANES), F32)
@@ -548,18 +557,20 @@
         moved=field_bytes,
     )
     recv = swap(send, "tile")
-    (mixed_own,) = call(
+    mixed_own, grad_act = call(
         functools.partial(own_body, edge=edge),
         (slots,),
         [
             scalar(slot_tiles),
             (ocean_fields, (1, edge, edge, channels), lambda s: (s, 0, 0, 0)),
             whole(depth_kernel),
+            by_slot(cot_rows, channels),
+            whole(reduce_weight),
         ],
-        [tile_out],
+        [tile_out, ((cells, hidden), F32, (area, hidden), lambda s: (s, 0))],
         [padded_scratch, taps],
         flops=mlp_flops,
-        moved=2 * field_bytes,
+        moved=6 * field_bytes,
     )
     next_rows, padded, grad_rows, weights, send = call(
         functools.partial(mlp_body, edge=edge, cap=cap),
@@ -570,9 +581,10 @@
             scalar(corner_sources),
             scalar(side_sends),
             scalar(corner_sends),
-            whole(recv),
+            placed(recv),
             whole(ocean_fields),
             (mixed_own, tile_block, lambda s: (s, 0, 0, 0, 0)),
+            by_slot(grad_act, hidden),
             by_slot(cot_rows, channels),
             whole(depth_kernel),
             whole(expand_weight),
@@ -613,7 +625,7 @@
             (padded, (1, groups, tall, wide, LANES), lambda s: (s, 0, 0, 0, 0)),
             by_slot(grad_rows, channels),
         ],
-        [((kernel_rows, channels), F32, (kernel_rows, channels), lambda s: (0, 0))],
+        [((kernel_rows, channels), BF16, (kernel_rows, channels), lambda s: (0, 0))],
         [padded_scratch, taps],
         flops=mlp_flops,
         moved=4 * field_bytes,
@@ -623,12 +635,13 @@
     mine = jnp.concatenate(
         [
             mine.reshape(tiles, part, channels),
-            kernel_part.astype(BF16).reshape(tiles, kernel_rows // tiles, channels),
+            kernel_part.reshape(tiles, kernel_rows // tiles, channels),
         ],
         axis=1,
     )
     blocks = swap(mine, "tile")
     half = slots // 2
+    device = lax.axis_index("basin").reshape(1)
 
     def final(first_slot, count, previous):
         rows_at = lambda s: (s + first_slot, 0)
@@ -636,7 +649,7 @@
             scalar(slot_tiles),
             scalar(side_sources),
             scalar(corner_sources),
-            whole(recv),
+            placed(recv),
             whole(grad_rows),
             (cot_rows, (area, channels), rows_at),
             whole(depth_kernel),
@@ -672,13 +685,13 @@
         ],
         axis=0,
     )
-    blocks, order = gather_blocks(mine, "basin")
+    blocks = gather_blocks(mine, "basin")
     grad_field = final(half, slots - half, grad_field)
     factor = 1.0 / math.sqrt(basins * tiles * cells)
     kernel_total, expand_total, reduce_total = call(
         functools.partial(weights_body, hidden=hidden, factor=factor),
         (1,),
-        [scalar(order)] + [whole(block) for block in blocks],
+        [scalar(device)] + [placed(block) for block in blocks],
         [
             ((TAPS, channels), F32, (TAPS, channels), lambda s: (0, 0)),
             ((channels, hidden), F32, (channels, hidden), lambda s: (0, 0)),
@@ -686,6 +699,7 @@
         ],
         [pltpu.VMEM((rows, channels), F32)],
         moved=6 * hidden * channels * 2,
+        limit=VMEM_LIMIT // 4,
     )
     shape = ocean_fields.shape
     return (

time: 145 us -> 139 us (0.959)
  local copies, waits for them, and re-layouts: 7.03 us -> 2.93 us
  other arithmetic: 2.67 us -> 1.18 us
    unnamed x14 -> x6, local copies, waits for them, and re-layouts: 5.82 us -> 1.72 us
  transfers between devices with their start and end apart: 8 -> 8, of which waited for: 3 -> 3; matrix products, arithmetic and copies ran while one was open for 1% -> 0% of each run, Pallas kernels for 29% -> 31%
where the time goes in v1:
time: 139 us; the launch traced here: 138 us
  Pallas kernels  68.6 us (49%)
  blocking collectives  28.4 us (20%)
  waiting for transfers between devices  23.1 us (17%)
  starting transfers between devices  13.4 us (10%)
  local copies, waits for them, and re-layouts  2.93 us (2%)
    pallas_call x7, Pallas kernels, call(): pl.pallas_call(body, grid=grid, in_specs=in_specs, out_specs=[pl.BlockSpe...  68.6 us
    all_to_all x2, blocking collectives, swap(): return lax.all_to_all(blocks, axis, split_axis=0, concat_axis=0, tiled=True)  28.4 us
    all_to_all x2, waiting for transfers between devices, swap(): return lax.all_to_all(blocks, axis, split_axis=0, concat_axis=0, tiled=True)  16.1 us
    all_to_all x2, starting transfers between devices, swap(): return lax.all_to_all(blocks, axis, split_axis=0, concat_axis=0, tiled=True)  11 us
    ppermute x1, waiting for transfers between devices, gather_blocks(): parts.append(lax.ppermute(block, axis, perm))  6.97 us
  transfers between devices with their start and end apart: 8, of which 3 were waited for; matrix products, arithmetic and copies ran while one was open for 0% of the time, Pallas kernels for 31%

profile of v1, /device:TPU:0, one launch (start us, length us, event | category | flops | bytes accessed | tf_op | source)
XLA Modules:
  0.0 138.4 jit_solution(13314492707723381854)
XLA Ops:
  0.6 2.6 %shard_map.137 = bf16[8,176,256]{2,1,0:T(8,128)(2,1)} custom-call(s32[4]{0:T(128)} %slot_ref.9, s32[2,8]{1,0:T(2,128)} %bitcast.30, s32[2,8]{1,0:T(2,128)} %bitcast.32, bf16[4,24,24,256]{3,2,1,0:T(8,128)(2,1)} %field.5), custom_call_target="tpu_custom_call" | custom-call | bytes 2359296 | tf_op jit(solution)/shard_map/pallas_call | solution.py:460
  3.3 7.3 %all-to-all-start = ((bf16[8,176,256]{2,1,0:T(8,128)(2,1)}), bf16[8,176,256]{2,1,0:T(8,128)(2,1)S(1)}, u32[]{:S(2)}, u32[]{:S(2)}) async-start(bf16[8,176,256]{2,1,0:T(8,128)(2,1)} %shard_map.137), calls=%async_computation | async-start | bytes 1441792 | tf_op jit(solution)/shard_map/all_to_all | solution.py:479
  10.6 12.7 %shard_map.138 = (f32[4,2,24,24,128]{4,3,2,1,0:T(8,128)}, f32[2304,1024]{1,0:T(8,128)}) custom-call(s32[4]{0:T(128)} %slot_ref.9, bf16[4,24,24,256]{3,2,1,0:T(8,128)(2,1)} %field.5, bf16[49,256]{1,0:T(8,128)(2,1)} %kernel_ref.7, bf16[2304,256]{1,0:T(8,128)(2,1)} %bitcast.34, bf16[1024,256]{1,0:T(8,128)(2,1)} %reduce.4), custom_call_target="tpu_custom_call" | custom-call | flops 3623878656 | bytes 14155776 | tf_op jit(solution)/shard_map/pallas_call | solution.py:460
  23.3 6.0 %all-to-all-done.recv = bf16[8,176,256]{2,1,0:T(8,128)(2,1)S(1)} async-done(((bf16[8,176,256]{2,1,0:T(8,128)(2,1)}), bf16[8,176,256]{2,1,0:T(8,128)(2,1)S(1)}, u32[]{:S(2)}, u32[]{:S(2)}) %all-to-all-start) | async-done | bytes 720928 | tf_op jit(solution)/shard_map/all_to_all | solution.py:479
  29.3 0.0 copy-start
  29.3 0.9 copy-done
  30.2 21.5 %shard_map.139 = (bf16[2304,256]{1,0:T(8,128)(2,1)}, f32[4,2,30,40,128]{4,3,2,1,0:T(8,128)}, bf16[2304,256]{1,0:T(8,128)(2,1)}, bf16[2048,256]{1,0:T(8,128)(2,1)}, bf16[8,176,256]{2,1,0:T(8,128)(2,1)}) custom-call(s32[4]{0:T(128)} %slot_ref.9, s32[4,4]{1,0:T(4,128)} %side_sources.5, s32[4,4]{1,0:T(4,128)} %corner_sources.5, s32[2,8]{1,0:T(2,128)} %bitcast.31, ...), custom_call_target="tpu_custom_call" | custom-call | flops 7247757312 | bytes 14155776 | tf_op jit(solution)/shard_map/pallas_call | solution.py:460
  51.7 1.2 dynamic-slice_bitcast_fusion.2
  52.9 0.1 collective-permute-start.2
  52.9 1.6 %collective-permute-start.1 = (bf16[512,256]{1,0:T(8,128)(2,1)S(1)}, bf16[512,256]{1,0:T(8,128)(2,1)S(1)}, u32[]{:S(2)}, u32[]{:S(2)}) collective-permute-start(bf16[512,256]{1,0:T(8,128)(2,1)S(1)} %get-tuple-element.27), channel_id=1, source_target_pairs={{0,16},{8,24},{16,0},{24,8},{1,17},{9,25},{17,1},{25,9},{2,18},{10... | collective-permute-start | bytes 786440 | tf_op jit(solution)/shard_map/ppermute | solution.py:489
  54.5 0.2 collective-permute-start
  54.6 13.5 %shard_map.142 = bf16[64,256]{1,0:T(8,128)(2,1)} custom-call(f32[4,2,30,40,128]{4,3,2,1,0:T(8,128)} %get-tuple-element.21.padded_field, bf16[2304,256]{1,0:T(8,128)(2,1)} %get-tuple-element.19.grad_ref), custom_call_target="tpu_custom_call" | custom-call | flops 3623878656 | bytes 9437184 | tf_op jit(solution)/shard_map/pallas_call | solution.py:460
  68.2 0.0 copy-start.2
  68.2 0.0 collective-permute-done.2
  68.2 0.0 collective-permute-done.1
  68.2 0.0 collective-permute-done
  68.2 1.1 fusion.2
  69.3 0.0 copy-done.2
  69.3 14.7 %all_to_all.20 = bf16[8,72,256]{2,1,0:T(8,128)(2,1)S(1)} all-to-all(bf16[8,72,256]{2,1,0:T(8,128)(2,1)S(1)} %pad_maximum_fusion), channel_id=1, replica_groups=mesh['basin'=4,'tile'=8] {'tile'}, dimensions={0} | all-to-all | bytes 589824 | tf_op jit(solution)/shard_map/all_to_all | solution.py:479
  84.1 13.7 %all_to_all.21 = bf16[8,72,256]{2,1,0:T(8,128)(2,1)S(1)} all-to-all(bf16[8,72,256]{2,1,0:T(8,128)(2,1)S(1)} %broadcast_in_dim.2), channel_id=1, replica_groups=mesh['basin'=4,'tile'=8] {'tile'}, dimensions={0} | all-to-all | bytes 589824 | tf_op jit(solution)/shard_map/all_to_all | solution.py:479
  97.8 3.7 %all-to-all-start.1 = ((bf16[8,176,256]{2,1,0:T(8,128)(2,1)}), bf16[8,176,256]{2,1,0:T(8,128)(2,1)S(1)}, u32[]{:S(2)}, u32[]{:S(2)}) async-start(bf16[8,176,256]{2,1,0:T(8,128)(2,1)} %get-tuple-element.18), calls=%async_computation.1 | async-start | bytes 1441792 | tf_op jit(solution)/shard_map/all_to_all | solution.py:479
  101.6 0.6 collective-permute-start.3
  102.2 0.0 collective-permute-start.4
  102.2 7.0 %collective-permute-done.3.refs_1_ = bf16[576,256]{1,0:T(8,128)(2,1)S(1)} collective-permute-done((bf16[576,256]{1,0:T(8,128)(2,1)S(1)}, bf16[576,256]{1,0:T(8,128)(2,1)S(1)}, u32[]{:S(2)}, u32[]{:S(2)}) %collective-permute-start.3) | collective-permute-done | bytes 294944 | tf_op jit(solution)/shard_map/ppermute | solution.py:499
  109.2 0.0 collective-permute-start.5
  109.2 10.2 %all-to-all-done.1.recv = bf16[8,176,256]{2,1,0:T(8,128)(2,1)S(1)} async-done(((bf16[8,176,256]{2,1,0:T(8,128)(2,1)}), bf16[8,176,256]{2,1,0:T(8,128)(2,1)S(1)}, u32[]{:S(2)}, u32[]{:S(2)}) %all-to-all-start.1) | async-done | bytes 720928 | tf_op jit(solution)/shard_map/all_to_all | solution.py:479
  119.4 0.0 copy-start.1
  119.4 0.9 copy-done.1
  120.2 8.3 %shard_map.140.rest_0_ = bf16[2304,256]{1,0:T(8,128)(2,1)} custom-call(s32[4]{0:T(128)} %slot_ref.9, s32[4,4]{1,0:T(4,128)} %side_sources.5, s32[4,4]{1,0:T(4,128)} %corner_sources.5, bf16[8,176,256]{2,1,0:T(8,128)(2,1)} %copy-done.1, bf16[2304,256]{1,0:T(8,128)(2,1)} %get-tuple-element.19.grad_ref, bf16[2304,256]{1,0:T(8,128)(2,1)} %bitcast.36, ...), custom_call_target="tpu_custom_call" | custom-call | flops 1811939328 | bytes 7077888 | tf_op jit(solution)/shard_map/pallas_call | solution.py:460
  128.5 8.3 %shard_map.141 = bf16[2304,256]{1,0:T(8,128)(2,1)} custom-call(s32[4]{0:T(128)} %slot_ref.9, s32[4,4]{1,0:T(4,128)} %side_sources.5, s32[4,4]{1,0:T(4,128)} %corner_sources.5, bf16[8,176,256]{2,1,0:T(8,128)(2,1)} %copy-done.1, bf16[2304,256]{1,0:T(8,128)(2,1)} %get-tuple-element.19.grad_ref, ...), custom_call_target="tpu_custom_call", output_to_operand_aliasing={{}: (7, {})} | custom-call | flops 1811939328 | bytes 7077888 | tf_op jit(solution)/shard_map/pallas_call | solution.py:460
  136.8 0.0 collective-permute-done.4.refs_2_
  136.8 0.0 collective-permute-done.5.refs_3_
  136.8 1.6 %shard_map.143 = (f32[49,256]{1,0:T(8,128)}, f32[256,1024]{1,0:T(8,128)}, f32[1024,256]{1,0:T(8,128)}) custom-call(s32[1]{0:T(128)} %bitcast.9.device, bf16[576,256]{1,0:T(8,128)(2,1)S(1)} %pad_maximum_fusion.1.refs_0_, bf16[576,256]{1,0:T(8,128)(2,1)S(1)} %collective-permute-done.3.refs_1_, bf16[576,256]{1,0:T(8,128)(2,1)S(1)} %collective-permute-done.4.refs_2_, ...), custom_call_target="tpu_custom_call" | custom-call | bytes 3145728 | tf_op jit(solution)/shard_map/pallas_call | solution.py:460
  (6 shorter events, 0.1 us)
Async XLA Ops:
  3.3 26.0 %all-to-all-start = ((bf16[8,176,256]{2,1,0:T(8,128)(2,1)}), bf16[8,176,256]{2,1,0:T(8,128)(2,1)S(1)}, u32[]{:S(2)}, u32[]{:S(2)}) async-start(bf16[8,176,256]{2,1,0:T(8,128)(2,1)} %shard_map.137), calls=%async_computation | async-start | bytes 1441792 | tf_op jit(solution)/shard_map/all_to_all | solution.py:479
  29.3 0.9 copy-start
  52.9 15.3 %collective-permute-start.2 = (bf16[512,256]{1,0:T(8,128)(2,1)S(1)}, bf16[512,256]{1,0:T(8,128)(2,1)S(1)}, u32[]{:S(2)}, u32[]{:S(2)}) collective-permute-start(bf16[512,256]{1,0:T(8,128)(2,1)S(1)} %get-tuple-element.26), channel_id=1, source_target_pairs={{0,24},{8,0},{16,8},{24,16},{1,25},{9,1},{17,9},{25,17},{2,26},{10... | collective-permute-start | bytes 786440 | tf_op jit(solution)/shard_map/ppermute | solution.py:489
  52.9 15.2 %collective-permute-start.1 = (bf16[512,256]{1,0:T(8,128)(2,1)S(1)}, bf16[512,256]{1,0:T(8,128)(2,1)S(1)}, u32[]{:S(2)}, u32[]{:S(2)}) collective-permute-start(bf16[512,256]{1,0:T(8,128)(2,1)S(1)} %get-tuple-element.27), channel_id=1, source_target_pairs={{0,16},{8,24},{16,0},{24,8},{1,17},{9,25},{17,1},{25,9},{2,18},{10... | collective-permute-start | bytes 786440 | tf_op jit(solution)/shard_map/ppermute | solution.py:489
  54.5 13.7 %collective-permute-start = (bf16[512,256]{1,0:T(8,128)(2,1)S(1)}, bf16[512,256]{1,0:T(8,128)(2,1)S(1)}, u32[]{:S(2)}, u32[]{:S(2)}) collective-permute-start(bf16[512,256]{1,0:T(8,128)(2,1)S(1)} %get-tuple-element.25), channel_id=1, source_target_pairs={{0,8},{8,16},{16,24},{24,0},{1,9},{9,17},{17,25},{25,1},{2,10},{10... | collective-permute-start | bytes 786440 | tf_op jit(solution)/shard_map/ppermute | solution.py:489
  68.2 1.1 copy-start.2
  97.8 21.5 %all-to-all-start.1 = ((bf16[8,176,256]{2,1,0:T(8,128)(2,1)}), bf16[8,176,256]{2,1,0:T(8,128)(2,1)S(1)}, u32[]{:S(2)}, u32[]{:S(2)}) async-start(bf16[8,176,256]{2,1,0:T(8,128)(2,1)} %get-tuple-element.18), calls=%async_computation.1 | async-start | bytes 1441792 | tf_op jit(solution)/shard_map/all_to_all | solution.py:479
  101.6 7.6 %collective-permute-start.3 = (bf16[576,256]{1,0:T(8,128)(2,1)S(1)}, bf16[576,256]{1,0:T(8,128)(2,1)S(1)}, u32[]{:S(2)}, u32[]{:S(2)}) collective-permute-start(bf16[576,256]{1,0:T(8,128)(2,1)S(1)} %pad_maximum_fusion.1.refs_0_), channel_id=1, source_target_pairs={{0,16},{8,24},{16,0},{24,8},{1,17},{9,25},{17,1},{25,9},{2,18},{10... | collective-permute-start | bytes 884744 | tf_op jit(solution)/shard_map/ppermute | solution.py:499
  102.2 34.6 %collective-permute-start.4 = (bf16[576,256]{1,0:T(8,128)(2,1)S(1)}, bf16[576,256]{1,0:T(8,128)(2,1)S(1)}, u32[]{:S(2)}, u32[]{:S(2)}) collective-permute-start(bf16[576,256]{1,0:T(8,128)(2,1)S(1)} %pad_maximum_fusion.1.refs_0_), channel_id=1, source_target_pairs={{0,8},{8,0},{16,24},{24,16},{1,9},{9,1},{17,25},{25,17},{2,10},{10... | collective-permute-start | bytes 884744 | tf_op jit(solution)/shard_map/ppermute | solution.py:500
  109.2 27.6 %collective-permute-start.5 = (bf16[576,256]{1,0:T(8,128)(2,1)S(1)}, bf16[576,256]{1,0:T(8,128)(2,1)S(1)}, u32[]{:S(2)}, u32[]{:S(2)}) collective-permute-start(bf16[576,256]{1,0:T(8,128)(2,1)S(1)} %collective-permute-done.3.refs_1_), channel_id=1, source_target_pairs={{0,8},{8,0},{16,24},{24,16},{1,9},{9,1},{17,25},{25,17},{2,10},{10... | collective-permute-start | bytes 884744 | tf_op jit(solution)/shard_map/ppermute | solution.py:500
  119.4 0.9 copy-start.1

commit v2 on v1

--- a/solution.py
+++ b/solution.py
@@ -401,7 +401,7 @@
     @pl.when(step == 0)
     def _():
         for grp in range(groups):
-            cells[grp] = grad_ref[:, grp * LANES : (grp + 1) * LANES].astype(F32)
+            cells[grp, : n_slots * area] = grad_ref[:, grp * LANES : (grp + 1) * LANES].astype(F32)
         side[zero_at] = jnp.zeros(side.shape[1:], F32)
         corner[zero_at] = jnp.zeros(corner.shape[1:], F32)
         received_records(recv, side, corner, cap)
@@ -535,7 +535,7 @@
     placed = lambda array: (array, None, pltpu.VMEM)
     by_slot = lambda array, width: (array, (area, width), lambda s: (s, 0))
     taps = pltpu.VMEM((groups, TAPS, 8, LANES), F32)
-    cell_scratch = pltpu.VMEM((groups, cells, LANES), F32)
+    cell_scratch = pltpu.VMEM((groups, cells + 8, LANES), F32)
     padded_scratch = pltpu.VMEM((groups, tall, wide, LANES), F32)
     own_side = pltpu.VMEM((4 * slots + 1, groups, n_side, LANES), F32)
     own_corner = pltpu.VMEM((4 * slots + 1, groups, n_corner, LANES), F32)
@@ -614,6 +614,7 @@
         ],
         flops=2 * mlp_flops,
         moved=6 * field_bytes,
+        limit=VMEM_LIMIT - 2 * 1024 * 1024,
     )
     recv = swap(send, "tile")
     rows = 2 * hidden

time: 139 us -> 138 us (level)
  no operation moved by 1% of the time
where the time goes in v2:
time: 138 us
  Pallas kernels  68.1 us (49%)
  blocking collectives  28.4 us (21%)
  waiting for transfers between devices  23.1 us (17%)
  starting transfers between devices  13.4 us (10%)
  local copies, waits for them, and re-layouts  2.93 us (2%)
    pallas_call x7, Pallas kernels, call(): pl.pallas_call(body, grid=grid, in_specs=in_specs, out_specs=[pl.BlockSpe...  68.1 us
    all_to_all x2, blocking collectives, swap(): return lax.all_to_all(blocks, axis, split_axis=0, concat_axis=0, tiled=True)  28.4 us
    all_to_all x2, waiting for transfers between devices, swap(): return lax.all_to_all(blocks, axis, split_axis=0, concat_axis=0, tiled=True)  16.1 us
    all_to_all x2, starting transfers between devices, swap(): return lax.all_to_all(blocks, axis, split_axis=0, concat_axis=0, tiled=True)  11 us
    ppermute x1, waiting for transfers between devices, gather_blocks(): parts.append(lax.ppermute(block, axis, perm))  6.98 us
  transfers between devices with their start and end apart: 8, of which 3 were waited for; matrix products, arithmetic and copies ran while one was open for 0% of the time, Pallas kernels for 31%

profile of v2, /device:TPU:0, one launch (start us, length us, event | category | flops | bytes accessed | tf_op | source)
XLA Modules:
  0.0 137.9 jit_solution(8887576204151376667)
XLA Ops:
  0.6 2.6 %shard_map.137 = bf16[8,176,256]{2,1,0:T(8,128)(2,1)} custom-call(s32[4]{0:T(128)} %slot_ref.9, s32[2,8]{1,0:T(2,128)} %bitcast.30, s32[2,8]{1,0:T(2,128)} %bitcast.32, bf16[4,24,24,256]{3,2,1,0:T(8,128)(2,1)} %field.5), custom_call_target="tpu_custom_call" | custom-call | bytes 2359296 | tf_op jit(solution)/shard_map/pallas_call | solution.py:460
  3.3 7.3 %all-to-all-start = ((bf16[8,176,256]{2,1,0:T(8,128)(2,1)}), bf16[8,176,256]{2,1,0:T(8,128)(2,1)S(1)}, u32[]{:S(2)}, u32[]{:S(2)}) async-start(bf16[8,176,256]{2,1,0:T(8,128)(2,1)} %shard_map.137), calls=%async_computation | async-start | bytes 1441792 | tf_op jit(solution)/shard_map/all_to_all | solution.py:479
  10.6 12.7 %shard_map.138 = (f32[4,2,24,24,128]{4,3,2,1,0:T(8,128)}, f32[2304,1024]{1,0:T(8,128)}) custom-call(s32[4]{0:T(128)} %slot_ref.9, bf16[4,24,24,256]{3,2,1,0:T(8,128)(2,1)} %field.5, bf16[49,256]{1,0:T(8,128)(2,1)} %kernel_ref.7, bf16[2304,256]{1,0:T(8,128)(2,1)} %bitcast.34, bf16[1024,256]{1,0:T(8,128)(2,1)} %reduce.4), custom_call_target="tpu_custom_call" | custom-call | flops 3623878656 | bytes 14155776 | tf_op jit(solution)/shard_map/pallas_call | solution.py:460
  23.3 6.0 %all-to-all-done.recv = bf16[8,176,256]{2,1,0:T(8,128)(2,1)S(1)} async-done(((bf16[8,176,256]{2,1,0:T(8,128)(2,1)}), bf16[8,176,256]{2,1,0:T(8,128)(2,1)S(1)}, u32[]{:S(2)}, u32[]{:S(2)}) %all-to-all-start) | async-done | bytes 720928 | tf_op jit(solution)/shard_map/all_to_all | solution.py:479
  29.3 0.0 copy-start
  29.3 0.9 copy-done
  30.2 21.5 %shard_map.139 = (bf16[2304,256]{1,0:T(8,128)(2,1)}, f32[4,2,30,40,128]{4,3,2,1,0:T(8,128)}, bf16[2304,256]{1,0:T(8,128)(2,1)}, bf16[2048,256]{1,0:T(8,128)(2,1)}, bf16[8,176,256]{2,1,0:T(8,128)(2,1)}) custom-call(s32[4]{0:T(128)} %slot_ref.9, s32[4,4]{1,0:T(4,128)} %side_sources.5, s32[4,4]{1,0:T(4,128)} %corner_sources.5, s32[2,8]{1,0:T(2,128)} %bitcast.31, ...), custom_call_target="tpu_custom_call" | custom-call | flops 7247757312 | bytes 14155776 | tf_op jit(solution)/shard_map/pallas_call | solution.py:460
  51.7 1.2 dynamic-slice_bitcast_fusion.2
  52.8 0.1 collective-permute-start.2
  52.9 1.6 %collective-permute-start.1 = (bf16[512,256]{1,0:T(8,128)(2,1)S(1)}, bf16[512,256]{1,0:T(8,128)(2,1)S(1)}, u32[]{:S(2)}, u32[]{:S(2)}) collective-permute-start(bf16[512,256]{1,0:T(8,128)(2,1)S(1)} %get-tuple-element.27), channel_id=1, source_target_pairs={{0,16},{8,24},{16,0},{24,8},{1,17},{9,25},{17,1},{25,9},{2,18},{10... | collective-permute-start | bytes 786440 | tf_op jit(solution)/shard_map/ppermute | solution.py:489
  54.5 0.2 collective-permute-start
  54.6 13.5 %shard_map.142 = bf16[64,256]{1,0:T(8,128)(2,1)} custom-call(f32[4,2,30,40,128]{4,3,2,1,0:T(8,128)} %get-tuple-element.21.padded_field, bf16[2304,256]{1,0:T(8,128)(2,1)} %get-tuple-element.19.grad_ref), custom_call_target="tpu_custom_call" | custom-call | flops 3623878656 | bytes 9437184 | tf_op jit(solution)/shard_map/pallas_call | solution.py:460
  68.1 0.0 copy-start.2
  68.1 0.0 collective-permute-done.2
  68.1 0.0 collective-permute-done.1
  68.1 0.0 collective-permute-done
  68.2 1.1 fusion.2
  69.2 0.0 copy-done.2
  69.3 14.7 %all_to_all.20 = bf16[8,72,256]{2,1,0:T(8,128)(2,1)S(1)} all-to-all(bf16[8,72,256]{2,1,0:T(8,128)(2,1)S(1)} %pad_maximum_fusion), channel_id=1, replica_groups=mesh['basin'=4,'tile'=8] {'tile'}, dimensions={0} | all-to-all | bytes 589824 | tf_op jit(solution)/shard_map/all_to_all | solution.py:479
  84.1 13.7 %all_to_all.21 = bf16[8,72,256]{2,1,0:T(8,128)(2,1)S(1)} all-to-all(bf16[8,72,256]{2,1,0:T(8,128)(2,1)S(1)} %broadcast_in_dim.2), channel_id=1, replica_groups=mesh['basin'=4,'tile'=8] {'tile'}, dimensions={0} | all-to-all | bytes 589824 | tf_op jit(solution)/shard_map/all_to_all | solution.py:479
  97.8 3.7 %all-to-all-start.1 = ((bf16[8,176,256]{2,1,0:T(8,128)(2,1)}), bf16[8,176,256]{2,1,0:T(8,128)(2,1)S(1)}, u32[]{:S(2)}, u32[]{:S(2)}) async-start(bf16[8,176,256]{2,1,0:T(8,128)(2,1)} %get-tuple-element.18), calls=%async_computation.1 | async-start | bytes 1441792 | tf_op jit(solution)/shard_map/all_to_all | solution.py:479
  101.6 0.6 collective-permute-start.3
  102.2 0.0 collective-permute-start.4
  102.2 7.0 %collective-permute-done.3.refs_1_ = bf16[576,256]{1,0:T(8,128)(2,1)S(1)} collective-permute-done((bf16[576,256]{1,0:T(8,128)(2,1)S(1)}, bf16[576,256]{1,0:T(8,128)(2,1)S(1)}, u32[]{:S(2)}, u32[]{:S(2)}) %collective-permute-start.3) | collective-permute-done | bytes 294944 | tf_op jit(solution)/shard_map/ppermute | solution.py:499
  109.2 0.0 collective-permute-start.5
  109.2 10.2 %all-to-all-done.1.recv = bf16[8,176,256]{2,1,0:T(8,128)(2,1)S(1)} async-done(((bf16[8,176,256]{2,1,0:T(8,128)(2,1)}), bf16[8,176,256]{2,1,0:T(8,128)(2,1)S(1)}, u32[]{:S(2)}, u32[]{:S(2)}) %all-to-all-start.1) | async-done | bytes 720928 | tf_op jit(solution)/shard_map/all_to_all | solution.py:479
  119.3 0.0 copy-start.1
  119.3 0.9 copy-done.1
  120.2 8.0 %shard_map.140.rest_0_ = bf16[2304,256]{1,0:T(8,128)(2,1)} custom-call(s32[4]{0:T(128)} %slot_ref.9, s32[4,4]{1,0:T(4,128)} %side_sources.5, s32[4,4]{1,0:T(4,128)} %corner_sources.5, bf16[8,176,256]{2,1,0:T(8,128)(2,1)} %copy-done.1, bf16[2304,256]{1,0:T(8,128)(2,1)} %get-tuple-element.19.grad_ref, bf16[2304,256]{1,0:T(8,128)(2,1)} %bitcast.36, ...), custom_call_target="tpu_custom_call" | custom-call | flops 1811939328 | bytes 7077888 | tf_op jit(solution)/shard_map/pallas_call | solution.py:460
  128.2 8.1 %shard_map.141 = bf16[2304,256]{1,0:T(8,128)(2,1)} custom-call(s32[4]{0:T(128)} %slot_ref.9, s32[4,4]{1,0:T(4,128)} %side_sources.5, s32[4,4]{1,0:T(4,128)} %corner_sources.5, bf16[8,176,256]{2,1,0:T(8,128)(2,1)} %copy-done.1, bf16[2304,256]{1,0:T(8,128)(2,1)} %get-tuple-element.19.grad_ref, ...), custom_call_target="tpu_custom_call", output_to_operand_aliasing={{}: (7, {})} | custom-call | flops 1811939328 | bytes 7077888 | tf_op jit(solution)/shard_map/pallas_call | solution.py:460
  136.3 0.0 collective-permute-done.4.refs_2_
  136.3 0.0 collective-permute-done.5.refs_3_
  136.3 1.6 %shard_map.143 = (f32[49,256]{1,0:T(8,128)}, f32[256,1024]{1,0:T(8,128)}, f32[1024,256]{1,0:T(8,128)}) custom-call(s32[1]{0:T(128)} %bitcast.9.device, bf16[576,256]{1,0:T(8,128)(2,1)S(1)} %pad_maximum_fusion.1.refs_0_, bf16[576,256]{1,0:T(8,128)(2,1)S(1)} %collective-permute-done.3.refs_1_, bf16[576,256]{1,0:T(8,128)(2,1)S(1)} %collective-permute-done.4.refs_2_, ...), custom_call_target="tpu_custom_call" | custom-call | bytes 3145728 | tf_op jit(solution)/shard_map/pallas_call | solution.py:460
  (6 shorter events, 0.1 us)
Async XLA Ops:
  3.3 26.0 %all-to-all-start = ((bf16[8,176,256]{2,1,0:T(8,128)(2,1)}), bf16[8,176,256]{2,1,0:T(8,128)(2,1)S(1)}, u32[]{:S(2)}, u32[]{:S(2)}) async-start(bf16[8,176,256]{2,1,0:T(8,128)(2,1)} %shard_map.137), calls=%async_computation | async-start | bytes 1441792 | tf_op jit(solution)/shard_map/all_to_all | solution.py:479
  29.3 0.9 copy-start
  52.8 15.3 %collective-permute-start.2 = (bf16[512,256]{1,0:T(8,128)(2,1)S(1)}, bf16[512,256]{1,0:T(8,128)(2,1)S(1)}, u32[]{:S(2)}, u32[]{:S(2)}) collective-permute-start(bf16[512,256]{1,0:T(8,128)(2,1)S(1)} %get-tuple-element.26), channel_id=1, source_target_pairs={{0,24},{8,0},{16,8},{24,16},{1,25},{9,1},{17,9},{25,17},{2,26},{10... | collective-permute-start | bytes 786440 | tf_op jit(solution)/shard_map/ppermute | solution.py:489
  52.9 15.2 %collective-permute-start.1 = (bf16[512,256]{1,0:T(8,128)(2,1)S(1)}, bf16[512,256]{1,0:T(8,128)(2,1)S(1)}, u32[]{:S(2)}, u32[]{:S(2)}) collective-permute-start(bf16[512,256]{1,0:T(8,128)(2,1)S(1)} %get-tuple-element.27), channel_id=1, source_target_pairs={{0,16},{8,24},{16,0},{24,8},{1,17},{9,25},{17,1},{25,9},{2,18},{10... | collective-permute-start | bytes 786440 | tf_op jit(solution)/shard_map/ppermute | solution.py:489
  54.5 13.7 %collective-permute-start = (bf16[512,256]{1,0:T(8,128)(2,1)S(1)}, bf16[512,256]{1,0:T(8,128)(2,1)S(1)}, u32[]{:S(2)}, u32[]{:S(2)}) collective-permute-start(bf16[512,256]{1,0:T(8,128)(2,1)S(1)} %get-tuple-element.25), channel_id=1, source_target_pairs={{0,8},{8,16},{16,24},{24,0},{1,9},{9,17},{17,25},{25,1},{2,10},{10... | collective-permute-start | bytes 786440 | tf_op jit(solution)/shard_map/ppermute | solution.py:489
  68.1 1.1 copy-start.2
  97.8 21.5 %all-to-all-start.1 = ((bf16[8,176,256]{2,1,0:T(8,128)(2,1)}), bf16[8,176,256]{2,1,0:T(8,128)(2,1)S(1)}, u32[]{:S(2)}, u32[]{:S(2)}) async-start(bf16[8,176,256]{2,1,0:T(8,128)(2,1)} %get-tuple-element.18), calls=%async_computation.1 | async-start | bytes 1441792 | tf_op jit(solution)/shard_map/all_to_all | solution.py:479
  101.6 7.6 %collective-permute-start.3 = (bf16[576,256]{1,0:T(8,128)(2,1)S(1)}, bf16[576,256]{1,0:T(8,128)(2,1)S(1)}, u32[]{:S(2)}, u32[]{:S(2)}) collective-permute-start(bf16[576,256]{1,0:T(8,128)(2,1)S(1)} %pad_maximum_fusion.1.refs_0_), channel_id=1, source_target_pairs={{0,16},{8,24},{16,0},{24,8},{1,17},{9,25},{17,1},{25,9},{2,18},{10... | collective-permute-start | bytes 884744 | tf_op jit(solution)/shard_map/ppermute | solution.py:499
  102.2 34.1 %collective-permute-start.4 = (bf16[576,256]{1,0:T(8,128)(2,1)S(1)}, bf16[576,256]{1,0:T(8,128)(2,1)S(1)}, u32[]{:S(2)}, u32[]{:S(2)}) collective-permute-start(bf16[576,256]{1,0:T(8,128)(2,1)S(1)} %pad_maximum_fusion.1.refs_0_), channel_id=1, source_target_pairs={{0,8},{8,0},{16,24},{24,16},{1,9},{9,1},{17,25},{25,17},{2,10},{10... | collective-permute-start | bytes 884744 | tf_op jit(solution)/shard_map/ppermute | solution.py:500
  109.2 27.1 %collective-permute-start.5 = (bf16[576,256]{1,0:T(8,128)(2,1)S(1)}, bf16[576,256]{1,0:T(8,128)(2,1)S(1)}, u32[]{:S(2)}, u32[]{:S(2)}) collective-permute-start(bf16[576,256]{1,0:T(8,128)(2,1)S(1)} %collective-permute-done.3.refs_1_), channel_id=1, source_target_pairs={{0,8},{8,0},{16,24},{24,16},{1,9},{9,1},{17,25},{25,17},{2,10},{10... | collective-permute-start | bytes 884744 | tf_op jit(solution)/shard_map/ppermute | solution.py:500
  119.3 0.9 copy-start.1
